TPU v7x, 32 devices: a whole 2x2x4 slice. The times are simulated.
32 devices in a mesh: tm: 8 (over y, x, core), space: 4 (over z).
Axes of the slice: x: 2, y: 2, z: 4, core: 2. Of those that a mesh axis runs over, the one named last changes fastest.
Arguments:
- start_block: float32 [16, 32, 8192], P('tm', None, 'space'), as said below
- stiffness_tiles: float32 [16, 320, 128, 128], P('tm', 'space'), as said below
- tile_columns: int32 [16, 320], P('tm', 'space'), may hold values from 0 to 63, as said below
Outputs:
- ritz_basis: float32 [16, 32, 8192], P('tm', None, 'space')
- first_basis: float32 [16, 32, 8192], P('tm', None, 'space')
- ritz_matrix: float32 [32, 32], replicated
Inputs may be any that keep to these rules, and one draw needn't show every extreme that they name: `tile_columns`: in every slice, block row r has its 5 tiles listed together in row order; the first names column block r, the others distinct column blocks (r + o) mod 64 with 0 < |o| <= 8; in every slice some block row has o = -8 and o = 8. `stiffness_tiles`: real entries. `start_block`: real entries.
All inputs are finite; a program needn't handle non-finite values.
Results may differ from a plain program's by a relative error of at most 0.00018.
Values sent between devices are 32-bit elements; how exact they have to be, the bound alone decides.
No kernel may reach another device: no remote copies, remote signals or barrier semaphores. Data moves between devices by JAX's collectives and lax.ppermute only.
A program may use at most 192 MiB of HBM per device.

v0:
```python
import jax
import jax.numpy as jnp
from jax import lax
from jax.sharding import PartitionSpec as P

TILE = 128
TPR = 5
HB = 8
CENTER = 6.5
RADIUS = 3.5
INFLATION_FACTOR = 0.8
accurate = lax.Precision.HIGHEST


def with_halo(cells, sides, width, closed):
    for axis, dim in sides:
        count = lax.axis_size(axis)
        ends = count if closed else count - 1
        head = lax.slice_in_dim(cells, 0, width, axis=dim)
        tail = lax.slice_in_dim(cells, cells.shape[dim] - width, cells.shape[dim], axis=dim)
        cells = jnp.concatenate(
            [
                lax.ppermute(tail, axis, [(i, (i + 1) % count) for i in range(ends)]),
                cells,
                lax.ppermute(head, axis, [((i + 1) % count, i) for i in range(ends)]),
            ],
            axis=dim,
        )
    return cells


def spatial_component(wide_vectors, tile_groups, column_groups):
    slices, width, extended_points = wide_vectors.shape
    wide_blocks = extended_points // TILE
    out_blocks = tile_groups.shape[1] // TPR

    def one_slice(slice_vec, tile_set, col_list):
        picked = jnp.take(slice_vec.reshape(width, wide_blocks, TILE), col_list, axis=1)
        products = jnp.einsum("nrc,knc->knr", tile_set, picked, precision=accurate)
        return (
            products.reshape(width, out_blocks, TPR, TILE)
            .sum(axis=2)
            .reshape(width, out_blocks * TILE)
        )

    return jax.vmap(one_slice)(wide_vectors, tile_groups, column_groups)


def temporal_component(vectors, degree):
    near_slices = with_halo(vectors, (("tm", 0),), 1, False)
    return degree[:, None, None] * vectors - near_slices[:-2] - near_slices[2:]


def apply_operator(vectors, tile_groups, column_groups, degree):
    extended_points = with_halo(vectors, (("space", 2),), HB * TILE, True)
    return spatial_component(
        extended_points, tile_groups, column_groups
    ) + INFLATION_FACTOR * temporal_component(vectors, degree)


def chebyshev_filter(vectors, operator):
    previous = vectors
    current = (operator(vectors) - CENTER * vectors) / RADIUS
    for step in range(2):
        following = 2.0 * (operator(current) - CENTER * current) / RADIUS - previous
        previous, current = (current, following)
    return current


def gram_terms(left_block, right_block):
    return jnp.einsum("sjp,skp->jk", left_block, right_block, precision=accurate)


def inverse_factor(gram_matrix):
    cholesky_factor = jnp.linalg.cholesky(gram_matrix)
    identity = jnp.eye(gram_matrix.shape[0], dtype=jnp.float32)
    return lax.linalg.triangular_solve(cholesky_factor, identity, left_side=True, lower=True)


def mix_vectors(matrix, vectors):
    return jnp.einsum("jk,skp->sjp", matrix, vectors, precision=accurate)


def body(start_block, stiffness_tiles, tile_columns):
    slices = start_block.shape[0]
    local_points = start_block.shape[2]
    local_blocks = local_points // TILE
    first_block = lax.axis_index("space") * local_blocks
    blocks_all = lax.axis_size("space") * local_blocks
    column_groups = (tile_columns - first_block + HB) % blocks_all
    count_all = slices * local_points * lax.axis_size("tm") * lax.axis_size("space")
    slice_index = lax.axis_index("tm") * slices + jnp.arange(slices, dtype=jnp.int32)
    last_slice = lax.axis_size("tm") * slices - 1
    degree = (
        2.0
        - (slice_index == 0).astype(jnp.float32)
        - (slice_index == last_slice).astype(jnp.float32)
    )

    def operator(vectors):
        return apply_operator(vectors, stiffness_tiles, column_groups, degree)

    def run_filter(vectors):
        return chebyshev_filter(vectors, operator)

    filtered = run_filter(start_block)
    first_gram = lax.psum(gram_terms(filtered, filtered), ("tm", "space")) / count_all
    first_basis = mix_vectors(inverse_factor(first_gram), filtered)
    second = run_filter(first_basis)
    second_gram = lax.psum(gram_terms(second, second), ("tm", "space")) / count_all
    ritz_basis = mix_vectors(inverse_factor(second_gram), second)
    image_block = operator(ritz_basis)
    ritz_matrix = lax.psum(gram_terms(ritz_basis, image_block), ("tm", "space")) / count_all
    return (ritz_basis, first_basis, ritz_matrix)


def solution(mesh):
    placed = (P("tm", None, "space"), P("tm", "space", None, None), P("tm", "space"))
    return jax.shard_map(
        body,
        mesh=mesh,
        in_specs=placed,
        out_specs=(P("tm", None, "space"), P("tm", None, "space"), P()),
        check_vma=False,
    )
```

profile of v0, /device:TPU:0, one launch (start us, length us, event | category | flops | bytes accessed | tf_op | source)
XLA Modules:
  0.0 426.7 jit_solution(2295299034075395820)
XLA Ops:
  1.7 3.1 collective-permute-start
  4.8 2.1 collective-permute-start.1
  8.6 2.2 collective-permute-start.2
  14.0 4.2 collective-permute-done.1
  19.3 3.8 gather_fusion
  23.1 19.4 %fusion.12 = f32[2,80,32,128]{3,2,1,0:T(8,128)S(1)} fusion(f32[2,80,128,128]{3,2,1,0:T(8,128)} %param.9, f32[2,80,32,128]{3,2,1,0:T(8,128)} %bitcast.210, pred[2,80]{1,0:T(4,128)(4,1)S(1)} %get-tuple-element.22), kind=kOutput, calls=%fused_computation.19 | convolution fusion | flops 1007288320 | bytes 15728800 | tf_op jit(solution)/shard_map/vmap(nrc,knc->knr)/dot_general | solution.py:39
  46.4 2.7 collective-permute-start.5
  52.2 4.1 collective-permute-done.4
  56.3 3.6 collective-permute-done.5
  60.1 3.8 gather_fusion.1
  63.9 20.5 %fusion.10 = f32[2,80,32,128]{3,2,1,0:T(8,128)} fusion(f32[2,80,128,128]{3,2,1,0:T(8,128)} %param.9, f32[2,80,32,128]{3,2,1,0:T(8,128)} %bitcast.211, pred[2,80]{1,0:T(4,128)(4,1)S(1)} %get-tuple-element.22), kind=kOutput, calls=%fused_computation.17 | convolution fusion | flops 1007288320 | bytes 15728800 | tf_op jit(solution)/shard_map/vmap(nrc,knc->knr)/dot_general | solution.py:39
  84.3 2.1 reduce_sum.64
  88.1 3.5 collective-permute-start.9
  94.4 4.4 %collective-permute-done.8 = f32[2,32,1024]{2,1,0:T(8,128)S(1)} collective-permute-done((f32[2,32,1024]{2,1,0:T(8,128)S(1)}, f32[2,32,1024]{2,1,0:T(8,128)S(1)}, u32[]{:S(2)}, u32[]{:S(2)}) %collective-permute-start.8) | collective-permute-done | bytes 262176 | tf_op jit(solution)/shard_map/ppermute | solution.py:23
  98.8 2.5 collective-permute-done.9
  101.4 3.8 gather_fusion.2
  105.2 20.5 %fusion.8 = f32[2,80,32,128]{3,2,1,0:T(8,128)} fusion(f32[2,80,128,128]{3,2,1,0:T(8,128)} %param.9, f32[2,80,32,128]{3,2,1,0:T(8,128)} %bitcast.212, pred[2,80]{1,0:T(4,128)(4,1)S(1)} %get-tuple-element.22), kind=kOutput, calls=%fused_computation.15 | convolution fusion | flops 1007288320 | bytes 15728800 | tf_op jit(solution)/shard_map/vmap(nrc,knc->knr)/dot_general | solution.py:39
  125.6 2.1 reduce_sum.65
  128.6 40.3 %psum.21 = f32[32,32]{0,1:T(8,128)S(1)} all-reduce(f32[32,32]{0,1:T(8,128)S(1)} %convolution_bitcast_fusion.6), channel_id=1, replica_groups=mesh['tm'=8,'space'=4] {'tm','space'}, use_global_device_ids=true, to_apply=%region_3.5 | all-reduce | flops 1024 | bytes 8192 | tf_op jit(solution)/shard_map/psum | solution.py:107
  169.0 2.9 cholesky.44
  173.3 2.4 custom-call.23
  177.1 3.3 collective-permute-start.13
  181.2 2.0 collective-permute-start.14
  184.7 3.0 collective-permute-done.12
  187.7 2.1 collective-permute-done.13
  189.9 3.8 gather_fusion.3
  193.6 19.4 %fusion.6 = f32[2,80,32,128]{3,2,1,0:T(8,128)S(1)} fusion(f32[2,80,128,128]{3,2,1,0:T(8,128)} %param.9, f32[2,80,32,128]{3,2,1,0:T(8,128)} %bitcast.213, pred[2,80]{1,0:T(4,128)(4,1)S(1)} %get-tuple-element.22), kind=kOutput, calls=%fused_computation.13 | convolution fusion | flops 1007288320 | bytes 15728800 | tf_op jit(solution)/shard_map/vmap(nrc,knc->knr)/dot_general | solution.py:39
  216.9 2.7 collective-permute-start.17
  222.7 4.2 collective-permute-done.16
  226.8 2.6 collective-permute-done.17
  229.6 3.8 gather_fusion.4
  233.3 20.5 %fusion.4 = f32[2,80,32,128]{3,2,1,0:T(8,128)} fusion(f32[2,80,128,128]{3,2,1,0:T(8,128)} %param.9, f32[2,80,32,128]{3,2,1,0:T(8,128)} %bitcast.214, pred[2,80]{1,0:T(4,128)(4,1)S(1)} %get-tuple-element.22), kind=kOutput, calls=%fused_computation.11 | convolution fusion | flops 1007288320 | bytes 15728800 | tf_op jit(solution)/shard_map/vmap(nrc,knc->knr)/dot_general | solution.py:39
  253.8 2.1 reduce_sum.67
  258.0 3.0 collective-permute-start.21
  263.9 4.4 %collective-permute-done.20 = f32[2,32,1024]{2,1,0:T(8,128)S(1)} collective-permute-done((f32[2,32,1024]{2,1,0:T(8,128)S(1)}, f32[2,32,1024]{2,1,0:T(8,128)S(1)}, u32[]{:S(2)}, u32[]{:S(2)}) %collective-permute-start.20) | collective-permute-done | bytes 262176 | tf_op jit(solution)/shard_map/ppermute | solution.py:23
  268.3 3.2 collective-permute-done.21
  271.7 3.8 gather_fusion.5
  275.4 20.5 %fusion.2 = f32[2,80,32,128]{3,2,1,0:T(8,128)} fusion(f32[2,80,128,128]{3,2,1,0:T(8,128)} %param.9, f32[2,80,32,128]{3,2,1,0:T(8,128)} %bitcast.215, pred[2,80]{1,0:T(4,128)(4,1)S(1)} %get-tuple-element.22), kind=kOutput, calls=%fused_computation.9 | convolution fusion | flops 1007288320 | bytes 15728800 | tf_op jit(solution)/shard_map/vmap(nrc,knc->knr)/dot_general | solution.py:39
  295.9 2.1 reduce_sum.68
  298.8 39.3 %psum.22 = f32[32,32]{0,1:T(8,128)S(1)} all-reduce(f32[32,32]{0,1:T(8,128)S(1)} %convolution_bitcast_fusion.4), channel_id=1, replica_groups=mesh['tm'=8,'space'=4] {'tm','space'}, use_global_device_ids=true, to_apply=%region_9.13 | all-reduce | flops 1024 | bytes 8192 | tf_op jit(solution)/shard_map/psum | solution.py:110
  338.2 2.9 cholesky.55
  342.4 2.4 custom-call.27
  347.1 2.5 collective-permute-start.25
  353.3 3.6 collective-permute-done.24
  356.9 2.8 collective-permute-done.25
  359.8 3.8 gather_fusion.6
  363.6 19.4 %fusion = f32[2,80,32,128]{3,2,1,0:T(8,128)S(1)} fusion(f32[2,80,128,128]{3,2,1,0:T(8,128)} %param.9, f32[2,80,32,128]{3,2,1,0:T(8,128)} %bitcast.209, pred[2,80]{1,0:T(4,128)(4,1)S(1)} %get-tuple-element.22), kind=kOutput, calls=%fused_computation.7 | convolution fusion | flops 1007288320 | bytes 15728800 | tf_op jit(solution)/shard_map/vmap(nrc,knc->knr)/dot_general | solution.py:39
  386.0 39.8 %psum.23 = f32[32,32]{0,1:T(8,128)S(1)} all-reduce(f32[32,32]{0,1:T(8,128)S(1)} %convolution_bitcast_fusion.2), channel_id=1, replica_groups=mesh['tm'=8,'space'=4] {'tm','space'}, use_global_device_ids=true, to_apply=%region_11.15 | all-reduce | flops 1024 | bytes 8192 | tf_op jit(solution)/shard_map/psum | solution.py:113
  (95 shorter events, 48.6 us)
Async XLA Ops:
  1.7 12.3 %collective-permute-start = (f32[2,32,1024]{2,1,0:T(8,128)S(1)}, f32[2,32,1024]{2,1,0:T(8,128)S(1)}, u32[]{:S(2)}, u32[]{:S(2)}) collective-permute-start(f32[2,32,1024]{2,1,0:T(8,128)S(1)} %get-tuple-element.48), channel_id=1, source_target_pairs={{0,1},{1,2},{2,3},{3,0},{4,5},{5,6},{6,7},{7,4},{8,9},{9,10},{10,1... | collective-permute-start | bytes 786440 | tf_op jit(solution)/shard_map/ppermute | solution.py:23
  4.8 13.4 %collective-permute-start.1 = (f32[2,32,1024]{2,1,0:T(8,128)S(1)}, f32[2,32,1024]{2,1,0:T(8,128)S(1)}, u32[]{:S(2)}, u32[]{:S(2)}) collective-permute-start(f32[2,32,1024]{2,1,0:T(8,128)S(1)} %get-tuple-element.49), channel_id=1, source_target_pairs={{1,0},{2,1},{3,2},{0,3},{5,4},{6,5},{7,6},{4,7},{9,8},{10,9},{11,1... | collective-permute-start | bytes 786440 | tf_op jit(solution)/shard_map/ppermute | solution.py:25
  8.6 35.1 %collective-permute-start.2 = (f32[1,32,2048]{2,1,0:T(8,128)}, f32[1,32,2048]{2,1,0:T(8,128)}, u32[]{:S(2)}, u32[]{:S(2)}) collective-permute-start(f32[1,32,2048]{2,1,0:T(8,128)} %get-tuple-element.50), channel_id=1, source_target_pairs={{0,4},{4,8},{8,12},{12,16},{16,20},{20,24},{24,28},{1,5},{5,9},{9,... | collective-permute-start | bytes 786440 | tf_op jit(solution)/shard_map/ppermute | solution.py:23
  10.8 32.9 %collective-permute-start.3 = (f32[1,32,2048]{2,1,0:T(8,128)S(1)}, f32[1,32,2048]{2,1,0:T(8,128)}, u32[]{:S(2)}, u32[]{:S(2)}) collective-permute-start(f32[1,32,2048]{2,1,0:T(8,128)S(1)} %get-tuple-element.51), channel_id=1, source_target_pairs={{4,0},{8,4},{12,8},{16,12},{20,16},{24,20},{28,24},{5,1},{9,5},{13... | collective-permute-start | bytes 786440 | tf_op jit(solution)/shard_map/ppermute | solution.py:25
  42.5 1.2 copy-start.2
  45.2 11.1 %collective-permute-start.4 = (f32[2,32,1024]{2,1,0:T(8,128)S(1)}, f32[2,32,1024]{2,1,0:T(8,128)S(1)}, u32[]{:S(2)}, u32[]{:S(2)}) collective-permute-start(f32[2,32,1024]{2,1,0:T(8,128)S(1)} %get-tuple-element.46), channel_id=1, source_target_pairs={{0,1},{1,2},{2,3},{3,0},{4,5},{5,6},{6,7},{7,4},{8,9},{9,10},{10,1... | collective-permute-start | bytes 786440 | tf_op jit(solution)/shard_map/ppermute | solution.py:23
  46.4 13.6 %collective-permute-start.5 = (f32[2,32,1024]{2,1,0:T(8,128)S(1)}, f32[2,32,1024]{2,1,0:T(8,128)S(1)}, u32[]{:S(2)}, u32[]{:S(2)}) collective-permute-start(f32[2,32,1024]{2,1,0:T(8,128)S(1)} %get-tuple-element.47), channel_id=1, source_target_pairs={{1,0},{2,1},{3,2},{0,3},{5,4},{6,5},{7,6},{4,7},{9,8},{10,9},{11,1... | collective-permute-start | bytes 786440 | tf_op jit(solution)/shard_map/ppermute | solution.py:25
  49.1 37.3 %collective-permute-start.6 = (f32[1,32,2048]{2,1,0:T(8,128)S(1)}, f32[1,32,2048]{2,1,0:T(8,128)S(1)}, u32[]{:S(2)}, u32[]{:S(2)}) collective-permute-start(f32[1,32,2048]{2,1,0:T(8,128)S(1)} %get-tuple-element.44), channel_id=1, source_target_pairs={{0,4},{4,8},{8,12},{12,16},{16,20},{20,24},{24,28},{1,5},{5,9},{9,... | collective-permute-start | bytes 786440 | tf_op jit(solution)/shard_map/ppermute | solution.py:23
  50.4 36.0 %collective-permute-start.7 = (f32[1,32,2048]{2,1,0:T(8,128)S(1)}, f32[1,32,2048]{2,1,0:T(8,128)}, u32[]{:S(2)}, u32[]{:S(2)}) collective-permute-start(f32[1,32,2048]{2,1,0:T(8,128)S(1)} %get-tuple-element.45), channel_id=1, source_target_pairs={{4,0},{8,4},{12,8},{16,12},{20,16},{24,20},{28,24},{5,1},{9,5},{13... | collective-permute-start | bytes 786440 | tf_op jit(solution)/shard_map/ppermute | solution.py:25
  87.7 11.1 %collective-permute-start.8 = (f32[2,32,1024]{2,1,0:T(8,128)S(1)}, f32[2,32,1024]{2,1,0:T(8,128)S(1)}, u32[]{:S(2)}, u32[]{:S(2)}) collective-permute-start(f32[2,32,1024]{2,1,0:T(8,128)S(1)} %get-tuple-element.42), channel_id=1, source_target_pairs={{0,1},{1,2},{2,3},{3,0},{4,5},{5,6},{6,7},{7,4},{8,9},{9,10},{10,1... | collective-permute-start | bytes 786440 | tf_op jit(solution)/shard_map/ppermute | solution.py:23
  88.1 13.1 %collective-permute-start.9 = (f32[2,32,1024]{2,1,0:T(8,128)S(1)}, f32[2,32,1024]{2,1,0:T(8,128)S(1)}, u32[]{:S(2)}, u32[]{:S(2)}) collective-permute-start(f32[2,32,1024]{2,1,0:T(8,128)S(1)} %get-tuple-element.43), channel_id=1, source_target_pairs={{1,0},{2,1},{3,2},{0,3},{5,4},{6,5},{7,6},{4,7},{9,8},{10,9},{11,1... | collective-permute-start | bytes 786440 | tf_op jit(solution)/shard_map/ppermute | solution.py:25
  91.6 36.1 %collective-permute-start.10 = (f32[1,32,2048]{2,1,0:T(8,128)S(1)}, f32[1,32,2048]{2,1,0:T(8,128)S(1)}, u32[]{:S(2)}, u32[]{:S(2)}) collective-permute-start(f32[1,32,2048]{2,1,0:T(8,128)S(1)} %get-tuple-element.40), channel_id=1, source_target_pairs={{0,4},{4,8},{8,12},{12,16},{16,20},{20,24},{24,28},{1,5},{5,9},{9,... | collective-permute-start | bytes 786440 | tf_op jit(solution)/shard_map/ppermute | solution.py:23
  93.0 34.8 %collective-permute-start.11 = (f32[1,32,2048]{2,1,0:T(8,128)S(1)}, f32[1,32,2048]{2,1,0:T(8,128)S(1)}, u32[]{:S(2)}, u32[]{:S(2)}) collective-permute-start(f32[1,32,2048]{2,1,0:T(8,128)S(1)} %get-tuple-element.41), channel_id=1, source_target_pairs={{4,0},{8,4},{12,8},{16,12},{20,16},{24,20},{28,24},{5,1},{9,5},{13... | collective-permute-start | bytes 786440 | tf_op jit(solution)/shard_map/ppermute | solution.py:25
  176.5 79.4 %copy-start.1 = (f32[2,32,2048]{2,1,0:T(8,128)}, f32[2,32,2048]{2,1,0:T(8,128)S(1)}, u32[]{:S(2)}) copy-start(f32[2,32,2048]{2,1,0:T(8,128)S(1)} %convolution_bitcast_fusion.1) | copy-start | bytes 1572868
  176.6 11.1 %collective-permute-start.12 = (f32[2,32,1024]{2,1,0:T(8,128)S(1)}, f32[2,32,1024]{2,1,0:T(8,128)S(1)}, u32[]{:S(2)}, u32[]{:S(2)}) collective-permute-start(f32[2,32,1024]{2,1,0:T(8,128)S(1)} %get-tuple-element.36), channel_id=1, source_target_pairs={{0,1},{1,2},{2,3},{3,0},{4,5},{5,6},{6,7},{7,4},{8,9},{9,10},{10,1... | collective-permute-start | bytes 786440 | tf_op jit(solution)/shard_map/ppermute | solution.py:23
  177.1 12.6 %collective-permute-start.13 = (f32[2,32,1024]{2,1,0:T(8,128)S(1)}, f32[2,32,1024]{2,1,0:T(8,128)S(1)}, u32[]{:S(2)}, u32[]{:S(2)}) collective-permute-start(f32[2,32,1024]{2,1,0:T(8,128)S(1)} %get-tuple-element.37), channel_id=1, source_target_pairs={{1,0},{2,1},{3,2},{0,3},{5,4},{6,5},{7,6},{4,7},{9,8},{10,9},{11,1... | collective-permute-start | bytes 786440 | tf_op jit(solution)/shard_map/ppermute | solution.py:25
  181.2 33.0 %collective-permute-start.14 = (f32[1,32,2048]{2,1,0:T(8,128)}, f32[1,32,2048]{2,1,0:T(8,128)}, u32[]{:S(2)}, u32[]{:S(2)}) collective-permute-start(f32[1,32,2048]{2,1,0:T(8,128)} %get-tuple-element.38), channel_id=1, source_target_pairs={{0,4},{4,8},{8,12},{12,16},{16,20},{20,24},{24,28},{1,5},{5,9},{9,... | collective-permute-start | bytes 786440 | tf_op jit(solution)/shard_map/ppermute | solution.py:23
  183.2 31.0 %collective-permute-start.15 = (f32[1,32,2048]{2,1,0:T(8,128)S(1)}, f32[1,32,2048]{2,1,0:T(8,128)}, u32[]{:S(2)}, u32[]{:S(2)}) collective-permute-start(f32[1,32,2048]{2,1,0:T(8,128)S(1)} %get-tuple-element.39), channel_id=1, source_target_pairs={{4,0},{8,4},{12,8},{16,12},{20,16},{24,20},{28,24},{5,1},{9,5},{13... | collective-permute-start | bytes 786440 | tf_op jit(solution)/shard_map/ppermute | solution.py:25
  215.7 11.1 %collective-permute-start.16 = (f32[2,32,1024]{2,1,0:T(8,128)S(1)}, f32[2,32,1024]{2,1,0:T(8,128)S(1)}, u32[]{:S(2)}, u32[]{:S(2)}) collective-permute-start(f32[2,32,1024]{2,1,0:T(8,128)S(1)} %get-tuple-element.34), channel_id=1, source_target_pairs={{0,1},{1,2},{2,3},{3,0},{4,5},{5,6},{6,7},{7,4},{8,9},{9,10},{10,1... | collective-permute-start | bytes 786440 | tf_op jit(solution)/shard_map/ppermute | solution.py:23
  216.9 12.5 %collective-permute-start.17 = (f32[2,32,1024]{2,1,0:T(8,128)S(1)}, f32[2,32,1024]{2,1,0:T(8,128)S(1)}, u32[]{:S(2)}, u32[]{:S(2)}) collective-permute-start(f32[2,32,1024]{2,1,0:T(8,128)S(1)} %get-tuple-element.35), channel_id=1, source_target_pairs={{1,0},{2,1},{3,2},{0,3},{5,4},{6,5},{7,6},{4,7},{9,8},{10,9},{11,1... | collective-permute-start | bytes 786440 | tf_op jit(solution)/shard_map/ppermute | solution.py:25
  219.6 36.3 %collective-permute-start.18 = (f32[1,32,2048]{2,1,0:T(8,128)S(1)}, f32[1,32,2048]{2,1,0:T(8,128)S(1)}, u32[]{:S(2)}, u32[]{:S(2)}) collective-permute-start(f32[1,32,2048]{2,1,0:T(8,128)S(1)} %get-tuple-element.32), channel_id=1, source_target_pairs={{0,4},{4,8},{8,12},{12,16},{16,20},{20,24},{24,28},{1,5},{5,9},{9,... | collective-permute-start | bytes 786440 | tf_op jit(solution)/shard_map/ppermute | solution.py:23
  220.9 35.0 %collective-permute-start.19 = (f32[1,32,2048]{2,1,0:T(8,128)S(1)}, f32[1,32,2048]{2,1,0:T(8,128)}, u32[]{:S(2)}, u32[]{:S(2)}) collective-permute-start(f32[1,32,2048]{2,1,0:T(8,128)S(1)} %get-tuple-element.33), channel_id=1, source_target_pairs={{4,0},{8,4},{12,8},{16,12},{20,16},{24,20},{28,24},{5,1},{9,5},{13... | collective-permute-start | bytes 786440 | tf_op jit(solution)/shard_map/ppermute | solution.py:25
  257.2 11.1 %collective-permute-start.20 = (f32[2,32,1024]{2,1,0:T(8,128)S(1)}, f32[2,32,1024]{2,1,0:T(8,128)S(1)}, u32[]{:S(2)}, u32[]{:S(2)}) collective-permute-start(f32[2,32,1024]{2,1,0:T(8,128)S(1)} %get-tuple-element.30), channel_id=1, source_target_pairs={{0,1},{1,2},{2,3},{3,0},{4,5},{5,6},{6,7},{7,4},{8,9},{9,10},{10,1... | collective-permute-start | bytes 786440 | tf_op jit(solution)/shard_map/ppermute | solution.py:23
  258.0 13.5 %collective-permute-start.21 = (f32[2,32,1024]{2,1,0:T(8,128)S(1)}, f32[2,32,1024]{2,1,0:T(8,128)S(1)}, u32[]{:S(2)}, u32[]{:S(2)}) collective-permute-start(f32[2,32,1024]{2,1,0:T(8,128)S(1)} %get-tuple-element.31), channel_id=1, source_target_pairs={{1,0},{2,1},{3,2},{0,3},{5,4},{6,5},{7,6},{4,7},{9,8},{10,9},{11,1... | collective-permute-start | bytes 786440 | tf_op jit(solution)/shard_map/ppermute | solution.py:25
  261.1 36.9 %collective-permute-start.22 = (f32[1,32,2048]{2,1,0:T(8,128)S(1)}, f32[1,32,2048]{2,1,0:T(8,128)S(1)}, u32[]{:S(2)}, u32[]{:S(2)}) collective-permute-start(f32[1,32,2048]{2,1,0:T(8,128)S(1)} %get-tuple-element.28), channel_id=1, source_target_pairs={{0,4},{4,8},{8,12},{12,16},{16,20},{20,24},{24,28},{1,5},{5,9},{9,... | collective-permute-start | bytes 786440 | tf_op jit(solution)/shard_map/ppermute | solution.py:23
  262.4 35.6 %collective-permute-start.23 = (f32[1,32,2048]{2,1,0:T(8,128)S(1)}, f32[1,32,2048]{2,1,0:T(8,128)S(1)}, u32[]{:S(2)}, u32[]{:S(2)}) collective-permute-start(f32[1,32,2048]{2,1,0:T(8,128)S(1)} %get-tuple-element.29), channel_id=1, source_target_pairs={{4,0},{8,4},{12,8},{16,12},{20,16},{24,20},{28,24},{5,1},{9,5},{13... | collective-permute-start | bytes 786440 | tf_op jit(solution)/shard_map/ppermute | solution.py:25
  345.7 38.5 %copy-start = (f32[2,32,2048]{2,1,0:T(8,128)}, f32[2,32,2048]{2,1,0:T(8,128)S(1)}, u32[]{:S(2)}) copy-start(f32[2,32,2048]{2,1,0:T(8,128)S(1)} %convolution_bitcast_fusion) | copy-start | bytes 1572868
  345.8 11.1 %collective-permute-start.24 = (f32[2,32,1024]{2,1,0:T(8,128)S(1)}, f32[2,32,1024]{2,1,0:T(8,128)S(1)}, u32[]{:S(2)}, u32[]{:S(2)}) collective-permute-start(f32[2,32,1024]{2,1,0:T(8,128)S(1)} %get-tuple-element.26), channel_id=1, source_target_pairs={{0,1},{1,2},{2,3},{3,0},{4,5},{5,6},{6,7},{7,4},{8,9},{9,10},{10,1... | collective-permute-start | bytes 786440 | tf_op jit(solution)/shard_map/ppermute | solution.py:23
  347.1 12.6 %collective-permute-start.25 = (f32[2,32,1024]{2,1,0:T(8,128)S(1)}, f32[2,32,1024]{2,1,0:T(8,128)S(1)}, u32[]{:S(2)}, u32[]{:S(2)}) collective-permute-start(f32[2,32,1024]{2,1,0:T(8,128)S(1)} %get-tuple-element.27), channel_id=1, source_target_pairs={{1,0},{2,1},{3,2},{0,3},{5,4},{6,5},{7,6},{4,7},{9,8},{10,9},{11,1... | collective-permute-start | bytes 786440 | tf_op jit(solution)/shard_map/ppermute | solution.py:25
  350.5 33.7 %collective-permute-start.26 = (f32[1,32,2048]{2,1,0:T(8,128)}, f32[1,32,2048]{2,1,0:T(8,128)S(1)}, u32[]{:S(2)}, u32[]{:S(2)}) collective-permute-start(f32[1,32,2048]{2,1,0:T(8,128)} %get-tuple-element.24), channel_id=1, source_target_pairs={{0,4},{4,8},{8,12},{12,16},{16,20},{20,24},{24,28},{1,5},{5,9},{9,... | collective-permute-start | bytes 786440 | tf_op jit(solution)/shard_map/ppermute | solution.py:23
  351.8 32.4 %collective-permute-start.27 = (f32[1,32,2048]{2,1,0:T(8,128)}, f32[1,32,2048]{2,1,0:T(8,128)}, u32[]{:S(2)}, u32[]{:S(2)}) collective-permute-start(f32[1,32,2048]{2,1,0:T(8,128)} %get-tuple-element.25), channel_id=1, source_target_pairs={{4,0},{8,4},{12,8},{16,12},{20,16},{24,20},{28,24},{5,1},{9,5},{13... | collective-permute-start | bytes 786440 | tf_op jit(solution)/shard_map/ppermute | solution.py:25
where the time goes:
time: 435 us; the launch traced here: 427 us
  matrix products  145 us (33%)
  blocking collectives  119 us (27%)
  starting transfers between devices  49.8 us (11%)
  waiting for transfers between devices  45.7 us (11%)
  other arithmetic  33.7 us (8%)
  local copies, waits for them, and re-layouts  32.1 us (7%)
    dot_general x7, matrix products, one_slice(): products = jnp.einsum('nrc,knc->knr', tile_set, picked, precision=accurate)  140 us
    psum x1, blocking collectives, body(): lax.psum(gram_terms(filtered, filtered), ('tm', 'space')) / count_all  40.3 us
    psum x1, blocking collectives, body(): lax.psum(gram_terms(ritz_basis, image_block), ('tm', 'space')) / count_all  39.8 us
    psum x1, blocking collectives, body(): lax.psum(gram_terms(second, second), ('tm', 'space')) / count_all  39.3 us
    ppermute x14, starting transfers between devices, with_halo(): lax.ppermute(head, axis, [((i + 1) % count, i) for i in range(ends)])  30.5 us
    gather x8, local copies, waits for them, and re-layouts, one_slice(): jnp.take(slice_vec.reshape(width, wide_blocks, TILE), col_list, axis=1)  26.4 us
    ppermute x14, waiting for transfers between devices, with_halo(): lax.ppermute(tail, axis, [(i, (i + 1) % count) for i in range(ends)])  24.7 us
    ppermute x14, waiting for transfers between devices, with_halo(): lax.ppermute(head, axis, [((i + 1) % count, i) for i in range(ends)])  21.1 us
  transfers between devices with their start and end apart: 28, of which 14 were waited for; matrix products, arithmetic and copies ran while one was open for 43% of the time, Pallas kernels for 0%

commit v1 on v0

--- a/solution.py
+++ b/solution.py
@@ -104,7 +104,9 @@
         return chebyshev_filter(vectors, operator)
 
     filtered = run_filter(start_block)
-    first_gram = lax.psum(gram_terms(filtered, filtered), ("tm", "space")) / count_all
+    first_gram = (
+        jnp.sum(lax.all_gather(gram_terms(filtered, filtered), ("tm", "space")), axis=0) / count_all
+    )
     first_basis = mix_vectors(inverse_factor(first_gram), filtered)
     second = run_filter(first_basis)
     second_gram = lax.psum(gram_terms(second, second), ("tm", "space")) / count_all

time: 435 us -> 460 us (1.057)
  blocking collectives: 119 us -> 149 us
    all_gather x0 -> x1, blocking collectives: none -> 69.6 us  [body(): lax.all_gather(gram_terms(filtered, filtered), ('tm', 'space'))]
    psum x1 -> x0, blocking collectives: 40.3 us -> none  [body(): lax.psum(gram_terms(filtered, filtered), ('tm', 'space')) / count_all]
  transfers between devices with their start and end apart: 28 -> 28, of which waited for: 14 -> 14; matrix products, arithmetic and copies ran while one was open for 43% -> 41% of each run, Pallas kernels for 0% -> 0%
where the time goes in v1:
time: 460 us; the launch traced here: 452 us
  blocking collectives  149 us (32%)
  matrix products  145 us (32%)
  starting transfers between devices  49.8 us (11%)
  waiting for transfers between devices  41.5 us (9%)
  other arithmetic  33.8 us (7%)
  local copies, waits for them, and re-layouts  32.1 us (7%)
    dot_general x7, matrix products, one_slice(): products = jnp.einsum('nrc,knc->knr', tile_set, picked, precision=accurate)  140 us
    all_gather x1, blocking collectives, body(): lax.all_gather(gram_terms(filtered, filtered), ('tm', 'space'))  69.6 us
    psum x1, blocking collectives, body(): lax.psum(gram_terms(ritz_basis, image_block), ('tm', 'space')) / count_all  39.8 us
    psum x1, blocking collectives, body(): lax.psum(gram_terms(second, second), ('tm', 'space')) / count_all  39.4 us
    ppermute x14, starting transfers between devices, with_halo(): lax.ppermute(head, axis, [((i + 1) % count, i) for i in range(ends)])  32.8 us
    gather x8, local copies, waits for them, and re-layouts, one_slice(): jnp.take(slice_vec.reshape(width, wide_blocks, TILE), col_list, axis=1)  26.4 us
    ppermute x14, waiting for transfers between devices, with_halo(): lax.ppermute(tail, axis, [(i, (i + 1) % count) for i in range(ends)])  22 us
    ppermute x14, waiting for transfers between devices, with_halo(): lax.ppermute(head, axis, [((i + 1) % count, i) for i in range(ends)])  19.5 us
  transfers between devices with their start and end apart: 28, of which 14 were waited for; matrix products, arithmetic and copies ran while one was open for 41% of the time, Pallas kernels for 0%

profile of v1, /device:TPU:0, one launch (start us, length us, event | category | flops | bytes accessed | tf_op | source)
XLA Modules:
  0.0 452.1 jit_solution(8298048411117884415)
XLA Ops:
  1.7 3.1 collective-permute-start
  4.8 2.1 collective-permute-start.1
  6.9 1.8 fusion.113
  8.6 2.2 collective-permute-start.2
  14.0 4.2 collective-permute-done.1
  19.3 3.8 gather_fusion
  23.1 19.4 %fusion.12 = f32[2,80,32,128]{3,2,1,0:T(8,128)S(1)} fusion(f32[2,80,128,128]{3,2,1,0:T(8,128)} %param.9, f32[2,80,32,128]{3,2,1,0:T(8,128)} %bitcast.211, pred[2,80]{1,0:T(4,128)(4,1)S(1)} %get-tuple-element.22), kind=kOutput, calls=%fused_computation.19 | convolution fusion | flops 1007288320 | bytes 15728800 | tf_op jit(solution)/shard_map/vmap(nrc,knc->knr)/dot_general | solution.py:39
  46.4 2.7 collective-permute-start.5
  52.2 4.1 collective-permute-done.4
  56.3 3.6 collective-permute-done.5
  60.1 3.8 gather_fusion.1
  63.9 20.5 %fusion.10 = f32[2,80,32,128]{3,2,1,0:T(8,128)} fusion(f32[2,80,128,128]{3,2,1,0:T(8,128)} %param.9, f32[2,80,32,128]{3,2,1,0:T(8,128)} %bitcast.212, pred[2,80]{1,0:T(4,128)(4,1)S(1)} %get-tuple-element.22), kind=kOutput, calls=%fused_computation.17 | convolution fusion | flops 1007288320 | bytes 15728800 | tf_op jit(solution)/shard_map/vmap(nrc,knc->knr)/dot_general | solution.py:39
  84.3 2.1 reduce_sum.73
  88.1 3.5 collective-permute-start.9
  94.4 4.4 collective-permute-done.8
  98.8 2.5 collective-permute-done.9
  101.4 3.8 gather_fusion.2
  105.2 20.5 %fusion.8 = f32[2,80,32,128]{3,2,1,0:T(8,128)} fusion(f32[2,80,128,128]{3,2,1,0:T(8,128)} %param.9, f32[2,80,32,128]{3,2,1,0:T(8,128)} %bitcast.213, pred[2,80]{1,0:T(4,128)(4,1)S(1)} %get-tuple-element.22), kind=kOutput, calls=%fused_computation.15 | convolution fusion | flops 1007288320 | bytes 15728800 | tf_op jit(solution)/shard_map/vmap(nrc,knc->knr)/dot_general | solution.py:39
  125.6 2.1 reduce_sum.74
  128.6 69.6 %all-gather = f32[1024,32]{1,0:T(8,128)S(1)} all-gather(f32[32,32]{1,0:T(8,128)S(1)} %convolution_bitcast_fusion.6), channel_id=2, replica_groups=mesh['tm'=8,'space'=4] {'tm','space'}, dimensions={0}, use_global_device_ids=true | all-gather | bytes 135168 | tf_op jit(solution)/shard_map/all_gather | solution.py:108
  198.4 2.9 cholesky.44
  202.7 2.4 custom-call.23
  206.2 3.7 collective-permute-start.13
  210.6 2.0 collective-permute-start.14
  215.5 3.8 gather_fusion.3
  219.2 19.4 %fusion.6 = f32[2,80,32,128]{3,2,1,0:T(8,128)S(1)} fusion(f32[2,80,128,128]{3,2,1,0:T(8,128)} %param.9, f32[2,80,32,128]{3,2,1,0:T(8,128)} %bitcast.214, pred[2,80]{1,0:T(4,128)(4,1)S(1)} %get-tuple-element.22), kind=kOutput, calls=%fused_computation.13 | convolution fusion | flops 1007288320 | bytes 15728800 | tf_op jit(solution)/shard_map/vmap(nrc,knc->knr)/dot_general | solution.py:39
  241.4 3.8 collective-permute-start.17
  248.3 4.2 collective-permute-done.16
  252.5 2.7 collective-permute-done.17
  255.3 3.8 gather_fusion.4
  259.1 20.5 %fusion.4 = f32[2,80,32,128]{3,2,1,0:T(8,128)} fusion(f32[2,80,128,128]{3,2,1,0:T(8,128)} %param.9, f32[2,80,32,128]{3,2,1,0:T(8,128)} %bitcast.215, pred[2,80]{1,0:T(4,128)(4,1)S(1)} %get-tuple-element.22), kind=kOutput, calls=%fused_computation.11 | convolution fusion | flops 1007288320 | bytes 15728800 | tf_op jit(solution)/shard_map/vmap(nrc,knc->knr)/dot_general | solution.py:39
  279.5 2.1 reduce_sum.77
  283.0 3.8 collective-permute-start.21
  289.6 4.4 collective-permute-done.20
  294.1 2.7 collective-permute-done.21
  296.9 3.8 gather_fusion.5
  300.7 20.5 %fusion.2 = f32[2,80,32,128]{3,2,1,0:T(8,128)} fusion(f32[2,80,128,128]{3,2,1,0:T(8,128)} %param.9, f32[2,80,32,128]{3,2,1,0:T(8,128)} %bitcast.216, pred[2,80]{1,0:T(4,128)(4,1)S(1)} %get-tuple-element.22), kind=kOutput, calls=%fused_computation.9 | convolution fusion | flops 1007288320 | bytes 15728800 | tf_op jit(solution)/shard_map/vmap(nrc,knc->knr)/dot_general | solution.py:39
  321.1 2.1 reduce_sum.78
  324.1 39.4 %psum.14 = f32[32,32]{0,1:T(8,128)S(1)} all-reduce(f32[32,32]{0,1:T(8,128)S(1)} %convolution_bitcast_fusion.4), channel_id=1, replica_groups=mesh['tm'=8,'space'=4] {'tm','space'}, use_global_device_ids=true, to_apply=%region_9.13 | all-reduce | flops 1024 | bytes 8192 | tf_op jit(solution)/shard_map/psum | solution.py:112
  363.6 2.9 cholesky.55
  367.9 2.4 custom-call.27
  372.5 2.6 collective-permute-start.25
  378.7 3.6 collective-permute-done.24
  382.3 2.8 collective-permute-done.25
  385.2 3.8 gather_fusion.6
  388.9 19.4 %fusion = f32[2,80,32,128]{3,2,1,0:T(8,128)S(1)} fusion(f32[2,80,128,128]{3,2,1,0:T(8,128)} %param.9, f32[2,80,32,128]{3,2,1,0:T(8,128)} %bitcast.210, pred[2,80]{1,0:T(4,128)(4,1)S(1)} %get-tuple-element.22), kind=kOutput, calls=%fused_computation.7 | convolution fusion | flops 1007288320 | bytes 15728800 | tf_op jit(solution)/shard_map/vmap(nrc,knc->knr)/dot_general | solution.py:39
  409.5 1.8 convolution_bitcast_fusion.2
  411.3 39.8 %psum.15 = f32[32,32]{0,1:T(8,128)S(1)} all-reduce(f32[32,32]{0,1:T(8,128)S(1)} %convolution_bitcast_fusion.2), channel_id=1, replica_groups=mesh['tm'=8,'space'=4] {'tm','space'}, use_global_device_ids=true, to_apply=%region_11.15 | all-reduce | flops 1024 | bytes 8192 | tf_op jit(solution)/shard_map/psum | solution.py:115
  (97 shorter events, 44.1 us)
Async XLA Ops:
  1.7 12.3 %collective-permute-start = (f32[2,32,1024]{2,1,0:T(8,128)S(1)}, f32[2,32,1024]{2,1,0:T(8,128)S(1)}, u32[]{:S(2)}, u32[]{:S(2)}) collective-permute-start(f32[2,32,1024]{2,1,0:T(8,128)S(1)} %get-tuple-element.48), channel_id=1, source_target_pairs={{0,1},{1,2},{2,3},{3,0},{4,5},{5,6},{6,7},{7,4},{8,9},{9,10},{10,1... | collective-permute-start | bytes 786440 | tf_op jit(solution)/shard_map/ppermute | solution.py:23
  4.8 13.4 %collective-permute-start.1 = (f32[2,32,1024]{2,1,0:T(8,128)S(1)}, f32[2,32,1024]{2,1,0:T(8,128)S(1)}, u32[]{:S(2)}, u32[]{:S(2)}) collective-permute-start(f32[2,32,1024]{2,1,0:T(8,128)S(1)} %get-tuple-element.49), channel_id=1, source_target_pairs={{1,0},{2,1},{3,2},{0,3},{5,4},{6,5},{7,6},{4,7},{9,8},{10,9},{11,1... | collective-permute-start | bytes 786440 | tf_op jit(solution)/shard_map/ppermute | solution.py:25
  8.6 35.1 %collective-permute-start.2 = (f32[1,32,2048]{2,1,0:T(8,128)}, f32[1,32,2048]{2,1,0:T(8,128)}, u32[]{:S(2)}, u32[]{:S(2)}) collective-permute-start(f32[1,32,2048]{2,1,0:T(8,128)} %get-tuple-element.50), channel_id=1, source_target_pairs={{0,4},{4,8},{8,12},{12,16},{16,20},{20,24},{24,28},{1,5},{5,9},{9,... | collective-permute-start | bytes 786440 | tf_op jit(solution)/shard_map/ppermute | solution.py:23
  10.8 32.9 %collective-permute-start.3 = (f32[1,32,2048]{2,1,0:T(8,128)S(1)}, f32[1,32,2048]{2,1,0:T(8,128)}, u32[]{:S(2)}, u32[]{:S(2)}) collective-permute-start(f32[1,32,2048]{2,1,0:T(8,128)S(1)} %get-tuple-element.51), channel_id=1, source_target_pairs={{4,0},{8,4},{12,8},{16,12},{20,16},{24,20},{28,24},{5,1},{9,5},{13... | collective-permute-start | bytes 786440 | tf_op jit(solution)/shard_map/ppermute | solution.py:25
  42.5 1.2 copy-start.2
  45.2 11.1 %collective-permute-start.4 = (f32[2,32,1024]{2,1,0:T(8,128)S(1)}, f32[2,32,1024]{2,1,0:T(8,128)S(1)}, u32[]{:S(2)}, u32[]{:S(2)}) collective-permute-start(f32[2,32,1024]{2,1,0:T(8,128)S(1)} %get-tuple-element.46), channel_id=1, source_target_pairs={{0,1},{1,2},{2,3},{3,0},{4,5},{5,6},{6,7},{7,4},{8,9},{9,10},{10,1... | collective-permute-start | bytes 786440 | tf_op jit(solution)/shard_map/ppermute | solution.py:23
  46.4 13.6 %collective-permute-start.5 = (f32[2,32,1024]{2,1,0:T(8,128)S(1)}, f32[2,32,1024]{2,1,0:T(8,128)S(1)}, u32[]{:S(2)}, u32[]{:S(2)}) collective-permute-start(f32[2,32,1024]{2,1,0:T(8,128)S(1)} %get-tuple-element.47), channel_id=1, source_target_pairs={{1,0},{2,1},{3,2},{0,3},{5,4},{6,5},{7,6},{4,7},{9,8},{10,9},{11,1... | collective-permute-start | bytes 786440 | tf_op jit(solution)/shard_map/ppermute | solution.py:25
  49.1 37.3 %collective-permute-start.6 = (f32[1,32,2048]{2,1,0:T(8,128)S(1)}, f32[1,32,2048]{2,1,0:T(8,128)S(1)}, u32[]{:S(2)}, u32[]{:S(2)}) collective-permute-start(f32[1,32,2048]{2,1,0:T(8,128)S(1)} %get-tuple-element.44), channel_id=1, source_target_pairs={{0,4},{4,8},{8,12},{12,16},{16,20},{20,24},{24,28},{1,5},{5,9},{9,... | collective-permute-start | bytes 786440 | tf_op jit(solution)/shard_map/ppermute | solution.py:23
  50.4 36.0 %collective-permute-start.7 = (f32[1,32,2048]{2,1,0:T(8,128)S(1)}, f32[1,32,2048]{2,1,0:T(8,128)}, u32[]{:S(2)}, u32[]{:S(2)}) collective-permute-start(f32[1,32,2048]{2,1,0:T(8,128)S(1)} %get-tuple-element.45), channel_id=1, source_target_pairs={{4,0},{8,4},{12,8},{16,12},{20,16},{24,20},{28,24},{5,1},{9,5},{13... | collective-permute-start | bytes 786440 | tf_op jit(solution)/shard_map/ppermute | solution.py:25
  87.7 11.1 %collective-permute-start.8 = (f32[2,32,1024]{2,1,0:T(8,128)S(1)}, f32[2,32,1024]{2,1,0:T(8,128)S(1)}, u32[]{:S(2)}, u32[]{:S(2)}) collective-permute-start(f32[2,32,1024]{2,1,0:T(8,128)S(1)} %get-tuple-element.42), channel_id=1, source_target_pairs={{0,1},{1,2},{2,3},{3,0},{4,5},{5,6},{6,7},{7,4},{8,9},{9,10},{10,1... | collective-permute-start | bytes 786440 | tf_op jit(solution)/shard_map/ppermute | solution.py:23
  88.1 13.1 %collective-permute-start.9 = (f32[2,32,1024]{2,1,0:T(8,128)S(1)}, f32[2,32,1024]{2,1,0:T(8,128)S(1)}, u32[]{:S(2)}, u32[]{:S(2)}) collective-permute-start(f32[2,32,1024]{2,1,0:T(8,128)S(1)} %get-tuple-element.43), channel_id=1, source_target_pairs={{1,0},{2,1},{3,2},{0,3},{5,4},{6,5},{7,6},{4,7},{9,8},{10,9},{11,1... | collective-permute-start | bytes 786440 | tf_op jit(solution)/shard_map/ppermute | solution.py:25
  91.6 36.1 %collective-permute-start.10 = (f32[1,32,2048]{2,1,0:T(8,128)S(1)}, f32[1,32,2048]{2,1,0:T(8,128)S(1)}, u32[]{:S(2)}, u32[]{:S(2)}) collective-permute-start(f32[1,32,2048]{2,1,0:T(8,128)S(1)} %get-tuple-element.40), channel_id=1, source_target_pairs={{0,4},{4,8},{8,12},{12,16},{16,20},{20,24},{24,28},{1,5},{5,9},{9,... | collective-permute-start | bytes 786440 | tf_op jit(solution)/shard_map/ppermute | solution.py:23
  93.0 34.8 %collective-permute-start.11 = (f32[1,32,2048]{2,1,0:T(8,128)S(1)}, f32[1,32,2048]{2,1,0:T(8,128)S(1)}, u32[]{:S(2)}, u32[]{:S(2)}) collective-permute-start(f32[1,32,2048]{2,1,0:T(8,128)S(1)} %get-tuple-element.41), channel_id=1, source_target_pairs={{4,0},{8,4},{12,8},{16,12},{20,16},{24,20},{28,24},{5,1},{9,5},{13... | collective-permute-start | bytes 786440 | tf_op jit(solution)/shard_map/ppermute | solution.py:25
  205.9 75.7 %copy-start.1 = (f32[2,32,2048]{2,1,0:T(8,128)}, f32[2,32,2048]{2,1,0:T(8,128)S(1)}, u32[]{:S(2)}) copy-start(f32[2,32,2048]{2,1,0:T(8,128)S(1)} %convolution_bitcast_fusion.1) | copy-start | bytes 1572868
  206.0 8.4 %collective-permute-start.12 = (f32[2,32,1024]{2,1,0:T(8,128)S(1)}, f32[2,32,1024]{2,1,0:T(8,128)S(1)}, u32[]{:S(2)}, u32[]{:S(2)}) collective-permute-start(f32[2,32,1024]{2,1,0:T(8,128)S(1)} %get-tuple-element.36), channel_id=1, source_target_pairs={{0,1},{1,2},{2,3},{3,0},{4,5},{5,6},{6,7},{7,4},{8,9},{9,10},{10,1... | collective-permute-start | bytes 786440 | tf_op jit(solution)/shard_map/ppermute | solution.py:23
  206.2 9.2 %collective-permute-start.13 = (f32[2,32,1024]{2,1,0:T(8,128)S(1)}, f32[2,32,1024]{2,1,0:T(8,128)S(1)}, u32[]{:S(2)}, u32[]{:S(2)}) collective-permute-start(f32[2,32,1024]{2,1,0:T(8,128)S(1)} %get-tuple-element.37), channel_id=1, source_target_pairs={{1,0},{2,1},{3,2},{0,3},{5,4},{6,5},{7,6},{4,7},{9,8},{10,9},{11,1... | collective-permute-start | bytes 786440 | tf_op jit(solution)/shard_map/ppermute | solution.py:25
  210.6 29.2 %collective-permute-start.14 = (f32[1,32,2048]{2,1,0:T(8,128)}, f32[1,32,2048]{2,1,0:T(8,128)}, u32[]{:S(2)}, u32[]{:S(2)}) collective-permute-start(f32[1,32,2048]{2,1,0:T(8,128)} %get-tuple-element.38), channel_id=1, source_target_pairs={{0,4},{4,8},{8,12},{12,16},{16,20},{20,24},{24,28},{1,5},{5,9},{9,... | collective-permute-start | bytes 786440 | tf_op jit(solution)/shard_map/ppermute | solution.py:23
  212.6 27.2 %collective-permute-start.15 = (f32[1,32,2048]{2,1,0:T(8,128)S(1)}, f32[1,32,2048]{2,1,0:T(8,128)}, u32[]{:S(2)}, u32[]{:S(2)}) collective-permute-start(f32[1,32,2048]{2,1,0:T(8,128)S(1)} %get-tuple-element.39), channel_id=1, source_target_pairs={{4,0},{8,4},{12,8},{16,12},{20,16},{24,20},{28,24},{5,1},{9,5},{13... | collective-permute-start | bytes 786440 | tf_op jit(solution)/shard_map/ppermute | solution.py:25
  241.3 11.1 %collective-permute-start.16 = (f32[2,32,1024]{2,1,0:T(8,128)S(1)}, f32[2,32,1024]{2,1,0:T(8,128)S(1)}, u32[]{:S(2)}, u32[]{:S(2)}) collective-permute-start(f32[2,32,1024]{2,1,0:T(8,128)S(1)} %get-tuple-element.34), channel_id=1, source_target_pairs={{0,1},{1,2},{2,3},{3,0},{4,5},{5,6},{6,7},{7,4},{8,9},{9,10},{10,1... | collective-permute-start | bytes 786440 | tf_op jit(solution)/shard_map/ppermute | solution.py:23
  241.4 13.7 %collective-permute-start.17 = (f32[2,32,1024]{2,1,0:T(8,128)S(1)}, f32[2,32,1024]{2,1,0:T(8,128)S(1)}, u32[]{:S(2)}, u32[]{:S(2)}) collective-permute-start(f32[2,32,1024]{2,1,0:T(8,128)S(1)} %get-tuple-element.35), channel_id=1, source_target_pairs={{1,0},{2,1},{3,2},{0,3},{5,4},{6,5},{7,6},{4,7},{9,8},{10,9},{11,1... | collective-permute-start | bytes 786440 | tf_op jit(solution)/shard_map/ppermute | solution.py:25
  245.2 36.4 %collective-permute-start.18 = (f32[1,32,2048]{2,1,0:T(8,128)S(1)}, f32[1,32,2048]{2,1,0:T(8,128)S(1)}, u32[]{:S(2)}, u32[]{:S(2)}) collective-permute-start(f32[1,32,2048]{2,1,0:T(8,128)S(1)} %get-tuple-element.32), channel_id=1, source_target_pairs={{0,4},{4,8},{8,12},{12,16},{16,20},{20,24},{24,28},{1,5},{5,9},{9,... | collective-permute-start | bytes 786440 | tf_op jit(solution)/shard_map/ppermute | solution.py:23
  246.6 35.1 %collective-permute-start.19 = (f32[1,32,2048]{2,1,0:T(8,128)S(1)}, f32[1,32,2048]{2,1,0:T(8,128)}, u32[]{:S(2)}, u32[]{:S(2)}) collective-permute-start(f32[1,32,2048]{2,1,0:T(8,128)S(1)} %get-tuple-element.33), channel_id=1, source_target_pairs={{4,0},{8,4},{12,8},{16,12},{20,16},{24,20},{28,24},{5,1},{9,5},{13... | collective-permute-start | bytes 786440 | tf_op jit(solution)/shard_map/ppermute | solution.py:25
  282.9 11.1 %collective-permute-start.20 = (f32[2,32,1024]{2,1,0:T(8,128)S(1)}, f32[2,32,1024]{2,1,0:T(8,128)S(1)}, u32[]{:S(2)}, u32[]{:S(2)}) collective-permute-start(f32[2,32,1024]{2,1,0:T(8,128)S(1)} %get-tuple-element.30), channel_id=1, source_target_pairs={{0,1},{1,2},{2,3},{3,0},{4,5},{5,6},{6,7},{7,4},{8,9},{9,10},{10,1... | collective-permute-start | bytes 786440 | tf_op jit(solution)/shard_map/ppermute | solution.py:23
  283.0 13.8 %collective-permute-start.21 = (f32[2,32,1024]{2,1,0:T(8,128)S(1)}, f32[2,32,1024]{2,1,0:T(8,128)S(1)}, u32[]{:S(2)}, u32[]{:S(2)}) collective-permute-start(f32[2,32,1024]{2,1,0:T(8,128)S(1)} %get-tuple-element.31), channel_id=1, source_target_pairs={{1,0},{2,1},{3,2},{0,3},{5,4},{6,5},{7,6},{4,7},{9,8},{10,9},{11,1... | collective-permute-start | bytes 786440 | tf_op jit(solution)/shard_map/ppermute | solution.py:25
  286.9 36.4 %collective-permute-start.22 = (f32[1,32,2048]{2,1,0:T(8,128)S(1)}, f32[1,32,2048]{2,1,0:T(8,128)S(1)}, u32[]{:S(2)}, u32[]{:S(2)}) collective-permute-start(f32[1,32,2048]{2,1,0:T(8,128)S(1)} %get-tuple-element.28), channel_id=1, source_target_pairs={{0,4},{4,8},{8,12},{12,16},{16,20},{20,24},{24,28},{1,5},{5,9},{9,... | collective-permute-start | bytes 786440 | tf_op jit(solution)/shard_map/ppermute | solution.py:23
  288.2 35.1 %collective-permute-start.23 = (f32[1,32,2048]{2,1,0:T(8,128)S(1)}, f32[1,32,2048]{2,1,0:T(8,128)S(1)}, u32[]{:S(2)}, u32[]{:S(2)}) collective-permute-start(f32[1,32,2048]{2,1,0:T(8,128)S(1)} %get-tuple-element.29), channel_id=1, source_target_pairs={{4,0},{8,4},{12,8},{16,12},{20,16},{24,20},{28,24},{5,1},{9,5},{13... | collective-permute-start | bytes 786440 | tf_op jit(solution)/shard_map/ppermute | solution.py:25
  371.1 38.4 %copy-start = (f32[2,32,2048]{2,1,0:T(8,128)}, f32[2,32,2048]{2,1,0:T(8,128)S(1)}, u32[]{:S(2)}) copy-start(f32[2,32,2048]{2,1,0:T(8,128)S(1)} %convolution_bitcast_fusion) | copy-start | bytes 1572868
  371.2 11.1 %collective-permute-start.24 = (f32[2,32,1024]{2,1,0:T(8,128)S(1)}, f32[2,32,1024]{2,1,0:T(8,128)S(1)}, u32[]{:S(2)}, u32[]{:S(2)}) collective-permute-start(f32[2,32,1024]{2,1,0:T(8,128)S(1)} %get-tuple-element.26), channel_id=1, source_target_pairs={{0,1},{1,2},{2,3},{3,0},{4,5},{5,6},{6,7},{7,4},{8,9},{9,10},{10,1... | collective-permute-start | bytes 786440 | tf_op jit(solution)/shard_map/ppermute | solution.py:23
  372.5 12.6 %collective-permute-start.25 = (f32[2,32,1024]{2,1,0:T(8,128)S(1)}, f32[2,32,1024]{2,1,0:T(8,128)S(1)}, u32[]{:S(2)}, u32[]{:S(2)}) collective-permute-start(f32[2,32,1024]{2,1,0:T(8,128)S(1)} %get-tuple-element.27), channel_id=1, source_target_pairs={{1,0},{2,1},{3,2},{0,3},{5,4},{6,5},{7,6},{4,7},{9,8},{10,9},{11,1... | collective-permute-start | bytes 786440 | tf_op jit(solution)/shard_map/ppermute | solution.py:25
  375.9 33.6 %collective-permute-start.26 = (f32[1,32,2048]{2,1,0:T(8,128)}, f32[1,32,2048]{2,1,0:T(8,128)S(1)}, u32[]{:S(2)}, u32[]{:S(2)}) collective-permute-start(f32[1,32,2048]{2,1,0:T(8,128)} %get-tuple-element.24), channel_id=1, source_target_pairs={{0,4},{4,8},{8,12},{12,16},{16,20},{20,24},{24,28},{1,5},{5,9},{9,... | collective-permute-start | bytes 786440 | tf_op jit(solution)/shard_map/ppermute | solution.py:23
  377.2 32.3 %collective-permute-start.27 = (f32[1,32,2048]{2,1,0:T(8,128)}, f32[1,32,2048]{2,1,0:T(8,128)}, u32[]{:S(2)}, u32[]{:S(2)}) collective-permute-start(f32[1,32,2048]{2,1,0:T(8,128)} %get-tuple-element.25), channel_id=1, source_target_pairs={{4,0},{8,4},{12,8},{16,12},{20,16},{24,20},{28,24},{5,1},{9,5},{13... | collective-permute-start | bytes 786440 | tf_op jit(solution)/shard_map/ppermute | solution.py:25
